TPU v7x, 512 devices: a whole 4x4x16 slice. The times are simulated.
512 devices in a mesh: test: 8 (over z_lo, core), bx: 4 (over y), by: 16 (over z_hi, x).
Axes of the slice: x: 4, y: 4, z: 16 (z_hi: 4, z_lo: 4; z = z_hi * 4 + z_lo), core: 2. Of those that a mesh axis runs over, the one named last changes fastest.
Arguments:
- log_conductivity: float32 [32, 128, 256], P('bx', 'by'), may hold values from -3 to 3
- storage: float32 [32, 128, 256], P('bx', 'by'), may hold values from 0.5 to 2
- recharge: float32 [32, 128, 256], P('bx', 'by'), may hold values from -6 to 6
- pump_rate: float32 [32], P('test'), may hold values from 4 to 16
- pump_well: int32 [32], P('test'), may hold values from 0 to 2047
- observed: float32 [32, 2048], P('test'), may hold values from -9 to 9
- owner: int32 [2048], replicated, may hold values from 0 to 63, as said below
- screen_column: int32 [2048], replicated, may hold values from 0 to 63
- screen_top: int32 [2048], replicated, may hold values from 0 to 248
Outputs:
- gradient: float32 [32, 128, 256], P('bx', 'by', 'test')
Inputs may be any that keep to these rules, and one draw needn't show every extreme that they name: `owner`: each brick owns exactly 32 wells.
All inputs are finite; a program needn't handle non-finite values.
Results may differ from a plain program's by a relative error of at most 0.0001.
Values sent between devices are 32-bit elements; how exact they have to be, the bound alone decides.
A program may use at most 64 MiB of HBM per device.

v0:
```python
import jax
import jax.numpy as jnp
from jax import lax
from jax.sharding import PartitionSpec as P

SWEEPS = 3
SCREEN = 8
epsilon = 1e-06


def with_halo(block, sides, width):
    for axis, dim in sides:
        count = lax.axis_size(axis)
        forward = [(i, i + 1) for i in range(count - 1)]
        backward = [(target, source) for source, target in forward]
        low = lax.ppermute(
            lax.slice_in_dim(block, block.shape[dim] - width, None, axis=dim), axis, forward
        )
        high = lax.ppermute(lax.slice_in_dim(block, 0, width, axis=dim), axis, backward)
        block = jnp.concatenate([low, block, high], axis=dim)
    return block


def pad_depth(values):
    return jnp.pad(values, [(0, 0)] * (values.ndim - 1) + [(1, 1)])


def neighbours(padded, centre):
    z_padded = pad_depth(centre)
    return [
        padded[..., 2:, 1:-1, :],
        padded[..., :-2, 1:-1, :],
        padded[..., 1:-1, 2:, :],
        padded[..., 1:-1, :-2, :],
        z_padded[..., 2:],
        z_padded[..., :-2],
    ]


def weighted(conductance, others):
    accumulated = conductance[0] * others[0]
    for position in range(1, 6):
        accumulated = accumulated + conductance[position] * others[position]
    return accumulated


def sensitivity(conductance, heads_field, heads_padded, adjoint_field, adjoint_padded):
    near_heads = neighbours(heads_padded, heads_field)
    near_adjoint = neighbours(adjoint_padded, adjoint_field)
    accumulated = jnp.zeros_like(heads_field)
    for position in range(6):
        accumulated = accumulated + conductance[position] * (heads_field - near_heads[position]) * (
            adjoint_field - near_adjoint[position]
        )
    return -0.5 * accumulated


def relax_field(source, conductance, diagonal):
    iterate = source / diagonal
    for sweep_index in range(SWEEPS - 1):
        padded = with_halo(iterate, (("bx", 1), ("by", 2)), 1)
        iterate = (source + weighted(conductance, neighbours(padded, iterate))) / diagonal
    return iterate


def per_sweep_terms(
    log_conductivity,
    storage,
    recharge,
    pump_rate,
    pump_well,
    observed,
    owner,
    screen_column,
    screen_top,
):
    size_x, size_y, size_z = log_conductivity.shape
    tests_here = pump_rate.shape[0]
    cell_count = size_x * size_y * size_z
    padded_log = with_halo(log_conductivity, (("bx", 0), ("by", 1)), 1)
    conductance = [
        jnp.exp(0.5 * (log_conductivity + other))
        for other in neighbours(padded_log, log_conductivity)
    ]
    diagonal = storage + weighted(conductance, [1.0] * 6)
    brick_index = lax.axis_index("bx") * lax.axis_size("by") + lax.axis_index("by")
    offsets = jnp.arange(SCREEN, dtype=jnp.int32)
    screen_cells = (screen_column * size_z + screen_top)[:, None] + offsets[None, :]
    owned_here = owner == brick_index
    pump_cells = screen_cells[pump_well]
    pump_value = jnp.where(owner[pump_well] == brick_index, -pump_rate, 0.0)
    test_rows = jnp.arange(tests_here, dtype=jnp.int32)[:, None]
    flat_source = jnp.broadcast_to(recharge.reshape(1, cell_count), (tests_here, cell_count))
    flat_source = flat_source.at[test_rows, pump_cells].add(
        jnp.broadcast_to(pump_value[:, None], pump_cells.shape)
    )
    source = flat_source.reshape(tests_here, size_x, size_y, size_z)
    heads_field = relax_field(source, conductance, diagonal)
    well_heads = jnp.mean(heads_field.reshape(tests_here, cell_count)[:, screen_cells], axis=2)
    residual = jnp.where(owned_here[None, :], well_heads - observed, 0.0)
    well_count = residual.shape[1]
    misfit = lax.psum(jnp.sum(residual * residual, axis=1), ("bx", "by")) / well_count + epsilon
    weights = residual / misfit[:, None]
    values = jnp.broadcast_to(weights[:, :, None], (tests_here, well_count, SCREEN)).reshape(
        tests_here, -1
    )
    adjoint_source = (
        jnp.zeros((tests_here, cell_count), jnp.float32).at[:, screen_cells.reshape(-1)].add(values)
    )
    adjoint_field = relax_field(
        adjoint_source.reshape(tests_here, size_x, size_y, size_z), conductance, diagonal
    )
    stacked = with_halo(
        jnp.concatenate([heads_field, adjoint_field], axis=0), (("bx", 1), ("by", 2)), 1
    )
    test_terms = sensitivity(
        conductance, heads_field, stacked[:tests_here], adjoint_field, stacked[tests_here:]
    )
    return (test_terms, misfit)


def local(
    log_conductivity,
    storage,
    recharge,
    pump_rate,
    pump_well,
    observed,
    owner,
    screen_column,
    screen_top,
):
    size_z = log_conductivity.shape[2]
    tests_here = pump_rate.shape[0]
    test_terms, misfit = per_sweep_terms(
        log_conductivity,
        storage,
        recharge,
        pump_rate,
        pump_well,
        observed,
        owner,
        screen_column,
        screen_top,
    )
    local_sum = jnp.sum(test_terms, axis=0)
    all_tests = tests_here * lax.axis_size("test")
    grand_total = lax.psum(local_sum, "test")
    slab_depth = size_z // lax.axis_size("test")
    gradient = lax.dynamic_slice_in_dim(
        grand_total, lax.axis_index("test") * slab_depth, slab_depth, 2
    )
    return gradient / all_tests


def solution(mesh):
    placed = (
        P("bx", "by", None),
        P("bx", "by", None),
        P("bx", "by", None),
        P("test"),
        P("test"),
        P("test", None),
        P(),
        P(),
        P(),
    )
    return jax.shard_map(
        local, mesh=mesh, in_specs=placed, out_specs=P("bx", "by", "test"), check_vma=False
    )
```

profile of v0, /device:TPU:2, one launch (start us, length us, event | category | flops | bytes accessed | tf_op | source)
XLA Modules:
  0.0 626.8 jit_solution(6473687219000279522)
XLA Ops:
  7.3 3.5 collective-permute-start.1
  10.7 1.3 collective-permute-start
  14.3 1.3 gather_fusion.1
  16.6 5.6 collective-permute-start.2
  22.2 1.9 collective-permute-start.3
  25.0 0.9 copy.25
  26.0 2.1 scatter_fusion
  28.1 1.2 add_add_fusion
  29.5 1.3 collective-permute-start.4
  30.8 5.2 collective-permute-start.5
  36.0 1.6 collective-permute-done.5
  37.6 3.9 collective-permute-start.6
  41.5 1.9 collective-permute-start.7
  44.3 3.1 collective-permute-done.7
  48.0 1.1 fusion.9
  49.1 1.3 collective-permute-start.8
  50.4 4.9 collective-permute-start.9
  55.3 1.5 collective-permute-done.9
  56.9 1.9 collective-permute-start.10
  58.8 4.6 collective-permute-start.11
  64.0 1.1 copy.21
  65.4 4.7 copy.20
  70.1 58.2 %gather_fusion.2 = f32[16384,4]{1,0:T(8,128)} fusion(f32[4,16384]{0,1:T(8,128)} %bitcast.34, s32[16384]{0:T(1024)S(1)} %broadcast_clamp_fusion), kind=kCustom, calls=%fused_computation.2 | custom fusion | bytes 589824 | tf_op jit(solution)/shard_map/gather | solution.py:99
  128.3 13.0 %bitcast_reduce_fusion = f32[2048,4]{1,0:T(8,128)S(1)} fusion(f32[16384,4]{1,0:T(8,128)} %gather_fusion.2), kind=kLoop, calls=%fused_computation.7 | loop fusion | flops 57344 | bytes 294912 | tf_op jit(solution)/shard_map/reduce_sum | solution.py:99
  142.5 236.4 %psum.14 = f32[4]{0:T(128)S(1)} all-reduce(f32[4]{0:T(128)S(1)} %multiply_reduce_fusion), channel_id=1, replica_groups=mesh['test'=8,'bx'=4,'by'=16] {'bx','by'}, use_global_device_ids=true, to_apply=%region_3.4 | all-reduce | flops 4 | bytes 32 | tf_op jit(solution)/shard_map/psum | solution.py:102
  379.4 91.6 %scatter_custom_fusion.1 = f32[4,16384]{0,1:T(8,128)} fusion(s32[16384]{0:T(1024)} %bitcast.41, f32[4,2048]{0,1:T(8,128)S(1)} %broadcast_divide_fusion, f32[]{:T(128)} %constant.27.clone.1), kind=kCustom, calls=%fused_computation.5 | custom fusion | flops 65536 | bytes 295424 | tf_op jit(solution)/shard_map/scatter-add | solution.py:108
  471.0 5.2 copy.24
  476.3 1.3 collective-permute-start.12
  477.6 4.5 collective-permute-start.13
  482.1 1.6 collective-permute-done.13
  483.8 4.0 collective-permute-start.14
  487.8 1.9 collective-permute-start.15
  489.7 4.0 collective-permute-done.15
  493.9 1.3 collective-permute-start.16
  495.2 4.9 collective-permute-start.17
  500.1 1.6 collective-permute-done.17
  501.7 1.9 collective-permute-start.18
  503.7 3.9 collective-permute-start.19
  507.6 1.9 collective-permute-done.19
  509.8 1.3 collective-permute-start.20
  511.1 4.9 collective-permute-start.21
  516.3 1.6 collective-permute-done.21
  518.0 1.9 collective-permute-start.22
  519.9 3.9 collective-permute-start.23
  524.3 1.9 collective-permute-done.23
  526.2 1.1 fusion.35
  527.4 91.2 %all-reduce.9.cloned.1.call-done = f32[8,8,256]{2,1,0:T(8,128)} async-done(((f32[8,8,256]{2,1,0:T(8,128)}), f32[8,8,256]{2,1,0:T(8,128)}) %all-reduce.9.cloned.1.call-update) | async-done | bytes 65552 | tf_op jit(solution)/shard_map/psum | solution.py:148
  618.5 1.4 dynamic-slice_multiply_fusion
  (83 shorter events, 10.5 us)
Async XLA Ops:
  6.5 56.9 %copy-start = (s32[2048]{0:T(1024)S(1)}, s32[2048]{0:T(1024)}, u32[]{:S(2)}) copy-start(s32[2048]{0:T(1024)} %param.15) | copy-start | bytes 24580
  6.5 612.0 %all-reduce.9.cloned.1.call-start = ((), (), s32[]{:S(2)}) async-start(), calls=%async_computation | async-start | bytes 131072 | tf_op jit(solution)/shard_map/psum | solution.py:148
  7.3 8.4 %collective-permute-start.1 = (f32[1,8,256]{2,1,0:T(8,128)S(1)}, f32[1,8,256]{2,1,0:T(8,128)S(1)}, u32[]{:S(2)}, u32[]{:S(2)}) collective-permute-start(f32[1,8,256]{2,1,0:T(8,128)S(1)} %get-tuple-element.35), channel_id=1, source_target_pairs={{0,16},{16,32},{32,48},{1,17},{17,33},{33,49},{2,18},{18,34},{34,5... | collective-permute-start | bytes 24584 | tf_op jit(solution)/shard_map/ppermute | solution.py:16
  10.7 5.8 collective-permute-start
  16.6 11.5 %collective-permute-start.2 = (f32[10,1,256]{2,1,0:T(1,128)S(1)}, f32[10,1,256]{2,1,0:T(1,128)S(1)}, u32[]{:S(2)}, u32[]{:S(2)}) collective-permute-start(f32[10,1,256]{2,1,0:T(1,128)S(1)} %get-tuple-element.33), channel_id=1, source_target_pairs={{1,0},{2,1},{3,2},{4,3},{5,4},{6,5},{7,6},{8,7},{9,8},{10,9},{11,1... | collective-permute-start | bytes 30728 | tf_op jit(solution)/shard_map/ppermute | solution.py:19
  22.2 5.9 collective-permute-start.3
  29.3 40.8 %copy-start.1 = (f32[8,8,256]{2,1,0:T(8,128)}, f32[8,8,256]{2,1,0:T(8,128)S(1)}, u32[]{:S(2)}) copy-start(f32[8,8,256]{2,1,0:T(8,128)S(1)} %get-tuple-element.7) | copy-start | bytes 196612
  29.3 40.8 %copy-start.3 = (f32[8,8,256]{2,1,0:T(8,128)}, f32[8,8,256]{2,1,0:T(8,128)S(1)}, u32[]{:S(2)}) copy-start(f32[8,8,256]{2,1,0:T(8,128)S(1)} %get-tuple-element.8) | copy-start | bytes 196612
  29.4 40.8 %copy-start.5 = (f32[8,8,256]{2,1,0:T(8,128)}, f32[8,8,256]{2,1,0:T(8,128)S(1)}, u32[]{:S(2)}) copy-start(f32[8,8,256]{2,1,0:T(8,128)S(1)} %get-tuple-element.9) | copy-start | bytes 196612
  29.4 40.8 %copy-start.7 = (f32[8,8,256]{2,1,0:T(8,128)}, f32[8,8,256]{2,1,0:T(8,128)S(1)}, u32[]{:S(2)}) copy-start(f32[8,8,256]{2,1,0:T(8,128)S(1)} %get-tuple-element.10) | copy-start | bytes 196612
  29.4 40.8 %copy-start.9 = (f32[8,8,256]{2,1,0:T(8,128)}, f32[8,8,256]{2,1,0:T(8,128)S(1)}, u32[]{:S(2)}) copy-start(f32[8,8,256]{2,1,0:T(8,128)S(1)} %get-tuple-element.11) | copy-start | bytes 196612
  29.5 6.5 %collective-permute-start.4 = (f32[4,1,8,256]{3,2,1,0:T(8,128)S(1)}, f32[4,1,8,256]{3,2,1,0:T(8,128)S(1)}, u32[]{:S(2)}, u32[]{:S(2)}) collective-permute-start(f32[4,1,8,256]{3,2,1,0:T(8,128)S(1)} %get-tuple-element.31), channel_id=1, source_target_pairs={{16,0},{32,16},{48,32},{17,1},{33,17},{49,33},{18,2},{34,18},{50,3... | collective-permute-start | bytes 98312 | tf_op jit(solution)/shard_map/ppermute | solution.py:19
  30.8 6.8 %collective-permute-start.5 = (f32[4,1,8,256]{3,2,1,0:T(8,128)S(1)}, f32[4,1,8,256]{3,2,1,0:T(8,128)S(1)}, u32[]{:S(2)}, u32[]{:S(2)}) collective-permute-start(f32[4,1,8,256]{3,2,1,0:T(8,128)S(1)} %get-tuple-element.30), channel_id=1, source_target_pairs={{0,16},{16,32},{32,48},{1,17},{17,33},{33,49},{2,18},{18,34},{34,5... | collective-permute-start | bytes 98312 | tf_op jit(solution)/shard_map/ppermute | solution.py:16
  37.6 6.7 %collective-permute-start.6 = (f32[4,10,1,256]{3,2,1,0:T(1,128)S(1)}, f32[4,10,1,256]{3,2,1,0:T(1,128)S(1)}, u32[]{:S(2)}, u32[]{:S(2)}) collective-permute-start(f32[4,10,1,256]{3,2,1,0:T(1,128)S(1)} %get-tuple-element.22), channel_id=1, source_target_pairs={{1,0},{2,1},{3,2},{4,3},{5,4},{6,5},{7,6},{8,7},{9,8},{10,9},{11,1... | collective-permute-start | bytes 122888 | tf_op jit(solution)/shard_map/ppermute | solution.py:19
  41.5 5.9 collective-permute-start.7
  44.3 3.1 copy-start.11
  47.4 0.6 copy-start.12
  49.1 6.2 collective-permute-start.8
  50.4 6.4 %collective-permute-start.9 = (f32[4,1,8,256]{3,2,1,0:T(8,128)S(1)}, f32[4,1,8,256]{3,2,1,0:T(8,128)S(1)}, u32[]{:S(2)}, u32[]{:S(2)}) collective-permute-start(f32[4,1,8,256]{3,2,1,0:T(8,128)S(1)} %get-tuple-element.28), channel_id=1, source_target_pairs={{0,16},{16,32},{32,48},{1,17},{17,33},{33,49},{2,18},{18,34},{34,5... | collective-permute-start | bytes 98312 | tf_op jit(solution)/shard_map/ppermute | solution.py:16
  56.9 8.2 %collective-permute-start.10 = (f32[4,10,1,256]{3,2,1,0:T(1,128)S(1)}, f32[4,10,1,256]{3,2,1,0:T(1,128)S(1)}, u32[]{:S(2)}, u32[]{:S(2)}) collective-permute-start(f32[4,10,1,256]{3,2,1,0:T(1,128)S(1)} %get-tuple-element.20), channel_id=1, source_target_pairs={{1,0},{2,1},{3,2},{4,3},{5,4},{6,5},{7,6},{8,7},{9,8},{10,9},{11,1... | collective-permute-start | bytes 122888 | tf_op jit(solution)/shard_map/ppermute | solution.py:19
  58.8 6.3 %collective-permute-start.11 = (f32[4,10,1,256]{3,2,1,0:T(1,128)S(1)}, f32[4,10,1,256]{3,2,1,0:T(1,128)S(1)}, u32[]{:S(2)}, u32[]{:S(2)}) collective-permute-start(f32[4,10,1,256]{3,2,1,0:T(1,128)S(1)} %get-tuple-element.21), channel_id=1, source_target_pairs={{0,1},{1,2},{2,3},{3,4},{4,5},{5,6},{6,7},{7,8},{8,9},{9,10},{10,1... | collective-permute-start | bytes 122888 | tf_op jit(solution)/shard_map/ppermute | solution.py:16
  379.4 114.3 %copy-start.2 = (f32[8,8,256]{2,1,0:T(8,128)S(1)}, f32[8,8,256]{2,1,0:T(8,128)}, u32[]{:S(2)}) copy-start(f32[8,8,256]{2,1,0:T(8,128)} %copy-done.1) | copy-start | bytes 196612
  379.4 114.3 %copy-start.4 = (f32[8,8,256]{2,1,0:T(8,128)S(1)}, f32[8,8,256]{2,1,0:T(8,128)}, u32[]{:S(2)}) copy-start(f32[8,8,256]{2,1,0:T(8,128)} %copy-done.3) | copy-start | bytes 196612
  379.4 114.3 %copy-start.6 = (f32[8,8,256]{2,1,0:T(8,128)S(1)}, f32[8,8,256]{2,1,0:T(8,128)}, u32[]{:S(2)}) copy-start(f32[8,8,256]{2,1,0:T(8,128)} %copy-done.5) | copy-start | bytes 196612
  379.4 114.3 %copy-start.8 = (f32[8,8,256]{2,1,0:T(8,128)S(1)}, f32[8,8,256]{2,1,0:T(8,128)}, u32[]{:S(2)}) copy-start(f32[8,8,256]{2,1,0:T(8,128)} %copy-done.7) | copy-start | bytes 196612
  379.4 114.3 %copy-start.10 = (f32[8,8,256]{2,1,0:T(8,128)S(1)}, f32[8,8,256]{2,1,0:T(8,128)}, u32[]{:S(2)}) copy-start(f32[8,8,256]{2,1,0:T(8,128)} %copy-done.9) | copy-start | bytes 196612
  476.3 5.9 collective-permute-start.12
  477.6 6.1 collective-permute-start.13
  483.8 5.9 collective-permute-start.14
  487.8 5.9 collective-permute-start.15
  493.9 6.2 collective-permute-start.16
  495.2 6.4 %collective-permute-start.17 = (f32[4,1,8,256]{3,2,1,0:T(8,128)S(1)}, f32[4,1,8,256]{3,2,1,0:T(8,128)S(1)}, u32[]{:S(2)}, u32[]{:S(2)}) collective-permute-start(f32[4,1,8,256]{3,2,1,0:T(8,128)S(1)} %get-tuple-element.24), channel_id=1, source_target_pairs={{0,16},{16,32},{32,48},{1,17},{17,33},{33,49},{2,18},{18,34},{34,5... | collective-permute-start | bytes 98312 | tf_op jit(solution)/shard_map/ppermute | solution.py:16
  501.7 5.9 collective-permute-start.18
  503.7 5.9 collective-permute-start.19
  509.8 6.5 %collective-permute-start.20 = (f32[8,1,8,256]{3,2,1,0:T(8,128)S(1)}, f32[8,1,8,256]{3,2,1,0:T(8,128)S(1)}, u32[]{:S(2)}, u32[]{:S(2)}) collective-permute-start(f32[8,1,8,256]{3,2,1,0:T(8,128)S(1)} %get-tuple-element.15), channel_id=1, source_target_pairs={{16,0},{32,16},{48,32},{17,1},{33,17},{49,33},{18,2},{34,18},{50,3... | collective-permute-start | bytes 196616 | tf_op jit(solution)/shard_map/ppermute | solution.py:19
  511.1 6.7 %collective-permute-start.21 = (f32[8,1,8,256]{3,2,1,0:T(8,128)S(1)}, f32[8,1,8,256]{3,2,1,0:T(8,128)S(1)}, u32[]{:S(2)}, u32[]{:S(2)}) collective-permute-start(f32[8,1,8,256]{3,2,1,0:T(8,128)S(1)} %get-tuple-element.14), channel_id=1, source_target_pairs={{0,16},{16,32},{32,48},{1,17},{17,33},{33,49},{2,18},{18,34},{34,5... | collective-permute-start | bytes 196616 | tf_op jit(solution)/shard_map/ppermute | solution.py:16
  518.0 6.3 %collective-permute-start.22 = (f32[8,10,1,256]{3,2,1,0:T(1,128)S(1)}, f32[8,10,1,256]{3,2,1,0:T(1,128)S(1)}, u32[]{:S(2)}, u32[]{:S(2)}) collective-permute-start(f32[8,10,1,256]{3,2,1,0:T(1,128)S(1)} %get-tuple-element.12), channel_id=1, source_target_pairs={{1,0},{2,1},{3,2},{4,3},{5,4},{6,5},{7,6},{8,7},{9,8},{10,9},{11,1... | collective-permute-start | bytes 245768 | tf_op jit(solution)/shard_map/ppermute | solution.py:19
  519.9 6.3 %collective-permute-start.23 = (f32[8,10,1,256]{3,2,1,0:T(1,128)S(1)}, f32[8,10,1,256]{3,2,1,0:T(1,128)S(1)}, u32[]{:S(2)}, u32[]{:S(2)}) collective-permute-start(f32[8,10,1,256]{3,2,1,0:T(1,128)S(1)} %get-tuple-element.13), channel_id=1, source_target_pairs={{0,1},{1,2},{2,3},{3,4},{4,5},{5,6},{6,7},{7,8},{8,9},{9,10},{10,1... | collective-permute-start | bytes 245768 | tf_op jit(solution)/shard_map/ppermute | solution.py:16
Sparse Core Ops, SparseCore 0:
  527.5 90.9 all-reduce.8
where the time goes:
time: 628 us; the launch traced here: 627 us
  blocking collectives  236 us (38%)
  other arithmetic  117 us (19%)
  waiting for transfers between devices  111 us (18%)
  local copies, waits for them, and re-layouts  75.6 us (12%)
  starting transfers between devices  73 us (12%)
  between operations  14 us (2%)
    psum x1, blocking collectives, per_sweep_terms(): lax.psum(jnp.sum(residual * residual, axis=1), ('bx', 'by')) / well_count  236 us
    scatter-add x1, other arithmetic, per_sweep_terms(): jnp.zeros((tests_here, cell_count), jnp.float32)  91.6 us
    psum x1, waiting for transfers between devices, local(): grand_total = lax.psum(local_sum, 'test')  91.2 us
    gather x1, local copies, waits for them, and re-layouts, per_sweep_terms(): heads_field.reshape(tests_here, cell_count)[:, screen_cells]  58.2 us
    ppermute x12, starting transfers between devices, with_halo(): lax.ppermute(lax.slice_in_dim(block, block.shape[dim] - width, None, axis...  45.9 us
    ppermute x12, starting transfers between devices, with_halo(): lax.ppermute(lax.slice_in_dim(block, 0, width, axis=dim), axis, backward)  27.1 us
    ppermute x12, waiting for transfers between devices, with_halo(): lax.ppermute(lax.slice_in_dim(block, block.shape[dim] - width, None, axis...  18.8 us
    reduce_sum x1, other arithmetic, per_sweep_terms(): jnp.mean(heads_field.reshape(tests_here, cell_count)[:, screen_cells], ax...  13 us
  transfers between devices with their start and end apart: 25, of which 12 were waited for; matrix products, arithmetic and copies ran while one was open for 2% of the time, Pallas kernels for 0%

commit v1 on v0

--- a/solution.py
+++ b/solution.py
@@ -145,7 +145,7 @@
     )
     local_sum = jnp.sum(test_terms, axis=0)
     all_tests = tests_here * lax.axis_size("test")
-    grand_total = lax.psum(local_sum, "test")
+    grand_total = jnp.sum(lax.all_gather(local_sum, "test"), axis=0)
     slab_depth = size_z // lax.axis_size("test")
     gradient = lax.dynamic_slice_in_dim(
         grand_total, lax.axis_index("test") * slab_depth, slab_depth, 2

time: 628 us -> 551 us (0.88)
  the two profiles are of different devices: /device:TPU:2 before, /device:TPU:153 now
where the time goes in v1:
time: 551 us; the launch traced here: 549 us
  blocking collectives  216 us (39%)
  other arithmetic  116 us (21%)
  starting transfers between devices  82 us (15%)
  local copies, waits for them, and re-layouts  75.3 us (14%)
  waiting for transfers between devices  60.1 us (11%)
    psum x1, blocking collectives, per_sweep_terms(): lax.psum(jnp.sum(residual * residual, axis=1), ('bx', 'by')) / well_count  157 us
    scatter-add x1, other arithmetic, per_sweep_terms(): jnp.zeros((tests_here, cell_count), jnp.float32)  91.6 us
    ppermute x12, waiting for transfers between devices, with_halo(): lax.ppermute(lax.slice_in_dim(block, block.shape[dim] - width, None, axis...  60.1 us
    ppermute x12, starting transfers between devices, with_halo(): lax.ppermute(lax.slice_in_dim(block, 0, width, axis=dim), axis, backward)  59 us
    all_gather x1, blocking collectives, local(): grand_total = jnp.sum(lax.all_gather(local_sum, 'test'), axis=0)  58.8 us
    gather x1, local copies, waits for them, and re-layouts, per_sweep_terms(): heads_field.reshape(tests_here, cell_count)[:, screen_cells]  57.9 us
    ppermute x12, starting transfers between devices, with_halo(): lax.ppermute(lax.slice_in_dim(block, block.shape[dim] - width, None, axis...  22.9 us
    reduce_sum x1, other arithmetic, per_sweep_terms(): jnp.mean(heads_field.reshape(tests_here, cell_count)[:, screen_cells], ax...  13 us
  transfers between devices with their start and end apart: 24, of which 11 were waited for; matrix products, arithmetic and copies ran while one was open for 2% of the time, Pallas kernels for 0%

profile of v1, /device:TPU:153, one launch (start us, length us, event | category | flops | bytes accessed | tf_op | source)
XLA Modules:
  0.0 549.4 jit_solution(4453964730085220216)
XLA Ops:
  0.7 1.3 collective-permute-start.1
  2.0 4.0 collective-permute-start
  8.3 1.3 gather_fusion.1
  10.5 2.6 collective-permute-start.2
  13.1 2.7 collective-permute-start.3
  16.7 0.9 copy.25
  17.7 2.1 scatter_fusion
  19.8 3.7 collective-permute-done.3
  23.5 1.2 add_add_fusion
  24.9 2.4 collective-permute-start.4
  27.2 1.3 collective-permute-start.5
  28.6 3.3 collective-permute-done.5
  32.0 4.9 collective-permute-start.6
  36.9 1.9 collective-permute-start.7
  39.6 8.0 %collective-permute-done.7 = f32[4,10,1,256]{3,2,1,0:T(1,128)S(1)} collective-permute-done((f32[4,10,1,256]{3,2,1,0:T(1,128)S(1)}, f32[4,10,1,256]{3,2,1,0:T(1,128)S(1)}, u32[]{:S(2)}, u32[]{:S(2)}) %collective-permute-start.7) | collective-permute-done | bytes 40992 | tf_op jit(solution)/shard_map/ppermute | solution.py:16
  48.2 1.1 fusion.9
  49.3 2.4 collective-permute-start.8
  51.7 1.3 collective-permute-start.9
  53.0 3.3 collective-permute-done.9
  56.4 1.9 collective-permute-start.10
  58.3 3.4 collective-permute-start.11
  62.2 1.1 copy.21
  63.4 5.7 %collective-permute-done.11 = f32[4,10,1,256]{3,2,1,0:T(1,128)S(1)} collective-permute-done((f32[4,10,1,256]{3,2,1,0:T(1,128)S(1)}, f32[4,10,1,256]{3,2,1,0:T(1,128)S(1)}, u32[]{:S(2)}, u32[]{:S(2)}) %collective-permute-start.11) | collective-permute-done | bytes 40992 | tf_op jit(solution)/shard_map/ppermute | solution.py:16
  69.4 4.7 copy.20
  74.1 57.9 %gather_fusion.2 = f32[16384,4]{1,0:T(8,128)} fusion(f32[4,16384]{0,1:T(8,128)} %bitcast.35, s32[16384]{0:T(1024)S(1)} %broadcast_clamp_fusion), kind=kCustom, calls=%fused_computation.2 | custom fusion | bytes 589824 | tf_op jit(solution)/shard_map/gather | solution.py:99
  132.0 13.0 %bitcast_reduce_fusion = f32[2048,4]{1,0:T(8,128)S(1)} fusion(f32[16384,4]{1,0:T(8,128)} %gather_fusion.2), kind=kLoop, calls=%fused_computation.7 | loop fusion | flops 57344 | bytes 294912 | tf_op jit(solution)/shard_map/reduce_sum | solution.py:99
  146.1 157.0 %psum.7 = f32[4]{0:T(128)S(1)} all-reduce(f32[4]{0:T(128)S(1)} %multiply_reduce_fusion), channel_id=1, replica_groups=mesh['test'=8,'bx'=4,'by'=16] {'bx','by'}, use_global_device_ids=true, to_apply=%region_3.4 | all-reduce | flops 4 | bytes 32 | tf_op jit(solution)/shard_map/psum | solution.py:102
  303.6 91.6 %scatter_custom_fusion.1 = f32[4,16384]{0,1:T(8,128)} fusion(s32[16384]{0:T(1024)} %bitcast.43, f32[4,2048]{0,1:T(8,128)S(1)} %broadcast_divide_fusion, f32[]{:T(128)} %constant.27.clone.1), kind=kCustom, calls=%fused_computation.5 | custom fusion | flops 65536 | bytes 295424 | tf_op jit(solution)/shard_map/scatter-add | solution.py:108
  395.2 5.2 copy.24
  400.5 1.8 collective-permute-start.12
  402.3 1.3 collective-permute-start.13
  403.7 3.3 collective-permute-done.13
  407.1 9.2 %collective-permute-start.14 = (f32[4,10,1,256]{3,2,1,0:T(1,128)S(1)}, f32[4,10,1,256]{3,2,1,0:T(1,128)S(1)}, u32[]{:S(2)}, u32[]{:S(2)}) collective-permute-start(f32[4,10,1,256]{3,2,1,0:T(1,128)S(1)} %get-tuple-element.18), channel_id=1, source_target_pairs={{1,0},{2,1},{3,2},{4,3},{5,4},{6,5},{7,6},{8,7},{9,8},{10,9},{11,1... | collective-permute-start | bytes 122888 | tf_op jit(solution)/shard_map/ppermute | solution.py:19
  416.3 1.9 collective-permute-start.15
  418.3 8.8 %collective-permute-done.15 = f32[4,10,1,256]{3,2,1,0:T(1,128)S(1)} collective-permute-done((f32[4,10,1,256]{3,2,1,0:T(1,128)S(1)}, f32[4,10,1,256]{3,2,1,0:T(1,128)S(1)}, u32[]{:S(2)}, u32[]{:S(2)}) %collective-permute-start.15) | collective-permute-done | bytes 40992 | tf_op jit(solution)/shard_map/ppermute | solution.py:16
  427.4 20.5 %collective-permute-start.16 = (f32[4,1,8,256]{3,2,1,0:T(8,128)S(1)}, f32[4,1,8,256]{3,2,1,0:T(8,128)S(1)}, u32[]{:S(2)}, u32[]{:S(2)}) collective-permute-start(f32[4,1,8,256]{3,2,1,0:T(8,128)S(1)} %get-tuple-element.25), channel_id=1, source_target_pairs={{16,0},{32,16},{48,32},{17,1},{33,17},{49,33},{18,2},{34,18},{50,3... | collective-permute-start | bytes 98312 | tf_op jit(solution)/shard_map/ppermute | solution.py:19
  447.9 1.3 collective-permute-start.17
  449.2 3.4 collective-permute-done.17
  452.6 4.0 collective-permute-start.18
  456.7 1.9 collective-permute-start.19
  458.6 8.8 %collective-permute-done.19 = f32[4,10,1,256]{3,2,1,0:T(1,128)S(1)} collective-permute-done((f32[4,10,1,256]{3,2,1,0:T(1,128)S(1)}, f32[4,10,1,256]{3,2,1,0:T(1,128)S(1)}, u32[]{:S(2)}, u32[]{:S(2)}) %collective-permute-start.19) | collective-permute-done | bytes 40992 | tf_op jit(solution)/shard_map/ppermute | solution.py:16
  467.7 3.4 collective-permute-start.20
  471.1 1.3 collective-permute-start.21
  472.4 3.7 collective-permute-done.21
  476.2 1.9 collective-permute-start.22
  478.1 3.4 collective-permute-start.23
  481.5 7.9 %collective-permute-done.23 = f32[8,10,1,256]{3,2,1,0:T(1,128)S(1)} collective-permute-done((f32[8,10,1,256]{3,2,1,0:T(1,128)S(1)}, f32[8,10,1,256]{3,2,1,0:T(1,128)S(1)}, u32[]{:S(2)}, u32[]{:S(2)}) %collective-permute-start.23) | collective-permute-done | bytes 81952 | tf_op jit(solution)/shard_map/ppermute | solution.py:16
  489.9 58.8 %all-gather = f32[64,8,256]{2,1,0:T(8,128)S(1)} all-gather(f32[8,8,256]{2,1,0:T(8,128)S(1)} %fusion.35), channel_id=2, replica_groups=mesh['test'=8,'bx'=4,'by'=16] {'test'}, dimensions={0}, use_global_device_ids=true | all-gather | bytes 589824 | tf_op jit(solution)/shard_map/all_gather | solution.py:148
  (82 shorter events, 10.9 us)
Async XLA Ops:
  0.0 61.7 %copy-start = (s32[2048]{0:T(1024)S(1)}, s32[2048]{0:T(1024)}, u32[]{:S(2)}) copy-start(s32[2048]{0:T(1024)} %param.15) | copy-start | bytes 24580
  0.7 8.9 %collective-permute-start.1 = (f32[1,8,256]{2,1,0:T(8,128)S(1)}, f32[1,8,256]{2,1,0:T(8,128)S(1)}, u32[]{:S(2)}, u32[]{:S(2)}) collective-permute-start(f32[1,8,256]{2,1,0:T(8,128)S(1)} %get-tuple-element.35), channel_id=1, source_target_pairs={{0,16},{16,32},{32,48},{1,17},{17,33},{33,49},{2,18},{18,34},{34,5... | collective-permute-start | bytes 24584 | tf_op jit(solution)/shard_map/ppermute | solution.py:16
  2.0 8.5 %collective-permute-start = (f32[1,8,256]{2,1,0:T(8,128)S(1)}, f32[1,8,256]{2,1,0:T(8,128)S(1)}, u32[]{:S(2)}, u32[]{:S(2)}) collective-permute-start(f32[1,8,256]{2,1,0:T(8,128)S(1)} %get-tuple-element.34), channel_id=1, source_target_pairs={{16,0},{32,16},{48,32},{17,1},{33,17},{49,33},{18,2},{34,18},{50,3... | collective-permute-start | bytes 24584 | tf_op jit(solution)/shard_map/ppermute | solution.py:19
  10.5 9.3 %collective-permute-start.2 = (f32[10,1,256]{2,1,0:T(1,128)S(1)}, f32[10,1,256]{2,1,0:T(1,128)S(1)}, u32[]{:S(2)}, u32[]{:S(2)}) collective-permute-start(f32[10,1,256]{2,1,0:T(1,128)S(1)} %get-tuple-element.33), channel_id=1, source_target_pairs={{1,0},{2,1},{3,2},{4,3},{5,4},{6,5},{7,6},{8,7},{9,8},{10,9},{11,1... | collective-permute-start | bytes 30728 | tf_op jit(solution)/shard_map/ppermute | solution.py:19
  13.1 10.4 %collective-permute-start.3 = (f32[10,1,256]{2,1,0:T(1,128)S(1)}, f32[10,1,256]{2,1,0:T(1,128)S(1)}, u32[]{:S(2)}, u32[]{:S(2)}) collective-permute-start(f32[10,1,256]{2,1,0:T(1,128)S(1)} %get-tuple-element.32), channel_id=1, source_target_pairs={{0,1},{1,2},{2,3},{3,4},{4,5},{5,6},{6,7},{7,8},{8,9},{9,10},{10,1... | collective-permute-start | bytes 30728 | tf_op jit(solution)/shard_map/ppermute | solution.py:16
  24.7 49.3 %copy-start.1 = (f32[8,8,256]{2,1,0:T(8,128)}, f32[8,8,256]{2,1,0:T(8,128)S(1)}, u32[]{:S(2)}) copy-start(f32[8,8,256]{2,1,0:T(8,128)S(1)} %get-tuple-element.7) | copy-start | bytes 196612
  24.8 49.3 %copy-start.3 = (f32[8,8,256]{2,1,0:T(8,128)}, f32[8,8,256]{2,1,0:T(8,128)S(1)}, u32[]{:S(2)}) copy-start(f32[8,8,256]{2,1,0:T(8,128)S(1)} %get-tuple-element.8) | copy-start | bytes 196612
  24.8 49.3 %copy-start.5 = (f32[8,8,256]{2,1,0:T(8,128)}, f32[8,8,256]{2,1,0:T(8,128)S(1)}, u32[]{:S(2)}) copy-start(f32[8,8,256]{2,1,0:T(8,128)S(1)} %get-tuple-element.9) | copy-start | bytes 196612
  24.8 49.3 %copy-start.7 = (f32[8,8,256]{2,1,0:T(8,128)}, f32[8,8,256]{2,1,0:T(8,128)S(1)}, u32[]{:S(2)}) copy-start(f32[8,8,256]{2,1,0:T(8,128)S(1)} %get-tuple-element.10) | copy-start | bytes 196612
  24.8 49.3 %copy-start.9 = (f32[8,8,256]{2,1,0:T(8,128)}, f32[8,8,256]{2,1,0:T(8,128)S(1)}, u32[]{:S(2)}) copy-start(f32[8,8,256]{2,1,0:T(8,128)S(1)} %get-tuple-element.11) | copy-start | bytes 196612
  24.9 3.7 collective-permute-start.4
  27.2 4.7 collective-permute-start.5
  32.0 7.7 %collective-permute-start.6 = (f32[4,10,1,256]{3,2,1,0:T(1,128)S(1)}, f32[4,10,1,256]{3,2,1,0:T(1,128)S(1)}, u32[]{:S(2)}, u32[]{:S(2)}) collective-permute-start(f32[4,10,1,256]{3,2,1,0:T(1,128)S(1)} %get-tuple-element.22), channel_id=1, source_target_pairs={{1,0},{2,1},{3,2},{4,3},{5,4},{6,5},{7,6},{8,7},{9,8},{10,9},{11,1... | collective-permute-start | bytes 122888 | tf_op jit(solution)/shard_map/ppermute | solution.py:19
  36.9 10.8 %collective-permute-start.7 = (f32[4,10,1,256]{3,2,1,0:T(1,128)S(1)}, f32[4,10,1,256]{3,2,1,0:T(1,128)S(1)}, u32[]{:S(2)}, u32[]{:S(2)}) collective-permute-start(f32[4,10,1,256]{3,2,1,0:T(1,128)S(1)} %get-tuple-element.23), channel_id=1, source_target_pairs={{0,1},{1,2},{2,3},{3,4},{4,5},{5,6},{6,7},{7,8},{8,9},{9,10},{10,1... | collective-permute-start | bytes 122888 | tf_op jit(solution)/shard_map/ppermute | solution.py:16
  39.6 8.0 %copy-start.11 = (f32[4,10,1,256]{3,2,1,0:T(1,128)}, f32[4,10,1,256]{3,2,1,0:T(1,128)S(1)}, u32[]{:S(2)}) copy-start(f32[4,10,1,256]{3,2,1,0:T(1,128)S(1)} %collective-permute-done.6) | copy-start | bytes 122884
  47.6 0.6 copy-start.12
  49.3 3.7 collective-permute-start.8
  51.7 4.7 collective-permute-start.9
  56.4 7.0 %collective-permute-start.10 = (f32[4,10,1,256]{3,2,1,0:T(1,128)S(1)}, f32[4,10,1,256]{3,2,1,0:T(1,128)S(1)}, u32[]{:S(2)}, u32[]{:S(2)}) collective-permute-start(f32[4,10,1,256]{3,2,1,0:T(1,128)S(1)} %get-tuple-element.20), channel_id=1, source_target_pairs={{1,0},{2,1},{3,2},{4,3},{5,4},{6,5},{7,6},{8,7},{9,8},{10,9},{11,1... | collective-permute-start | bytes 122888 | tf_op jit(solution)/shard_map/ppermute | solution.py:19
  58.3 10.8 %collective-permute-start.11 = (f32[4,10,1,256]{3,2,1,0:T(1,128)S(1)}, f32[4,10,1,256]{3,2,1,0:T(1,128)S(1)}, u32[]{:S(2)}, u32[]{:S(2)}) collective-permute-start(f32[4,10,1,256]{3,2,1,0:T(1,128)S(1)} %get-tuple-element.21), channel_id=1, source_target_pairs={{0,1},{1,2},{2,3},{3,4},{4,5},{5,6},{6,7},{7,8},{8,9},{9,10},{10,1... | collective-permute-start | bytes 122888 | tf_op jit(solution)/shard_map/ppermute | solution.py:16
  303.6 123.5 %copy-start.2 = (f32[8,8,256]{2,1,0:T(8,128)S(1)}, f32[8,8,256]{2,1,0:T(8,128)}, u32[]{:S(2)}) copy-start(f32[8,8,256]{2,1,0:T(8,128)} %copy-done.1) | copy-start | bytes 196612
  303.6 123.5 %copy-start.4 = (f32[8,8,256]{2,1,0:T(8,128)S(1)}, f32[8,8,256]{2,1,0:T(8,128)}, u32[]{:S(2)}) copy-start(f32[8,8,256]{2,1,0:T(8,128)} %copy-done.3) | copy-start | bytes 196612
  303.6 123.5 %copy-start.6 = (f32[8,8,256]{2,1,0:T(8,128)S(1)}, f32[8,8,256]{2,1,0:T(8,128)}, u32[]{:S(2)}) copy-start(f32[8,8,256]{2,1,0:T(8,128)} %copy-done.5) | copy-start | bytes 196612
  303.6 123.5 %copy-start.8 = (f32[8,8,256]{2,1,0:T(8,128)S(1)}, f32[8,8,256]{2,1,0:T(8,128)}, u32[]{:S(2)}) copy-start(f32[8,8,256]{2,1,0:T(8,128)} %copy-done.7) | copy-start | bytes 196612
  303.6 123.5 %copy-start.10 = (f32[8,8,256]{2,1,0:T(8,128)S(1)}, f32[8,8,256]{2,1,0:T(8,128)}, u32[]{:S(2)}) copy-start(f32[8,8,256]{2,1,0:T(8,128)} %copy-done.9) | copy-start | bytes 196612
  400.5 3.2 collective-permute-start.12
  402.3 4.7 collective-permute-start.13
  407.1 11.2 %collective-permute-start.14 = (f32[4,10,1,256]{3,2,1,0:T(1,128)S(1)}, f32[4,10,1,256]{3,2,1,0:T(1,128)S(1)}, u32[]{:S(2)}, u32[]{:S(2)}) collective-permute-start(f32[4,10,1,256]{3,2,1,0:T(1,128)S(1)} %get-tuple-element.18), channel_id=1, source_target_pairs={{1,0},{2,1},{3,2},{4,3},{5,4},{6,5},{7,6},{8,7},{9,8},{10,9},{11,1... | collective-permute-start | bytes 122888 | tf_op jit(solution)/shard_map/ppermute | solution.py:19
  416.3 10.8 %collective-permute-start.15 = (f32[4,10,1,256]{3,2,1,0:T(1,128)S(1)}, f32[4,10,1,256]{3,2,1,0:T(1,128)S(1)}, u32[]{:S(2)}, u32[]{:S(2)}) collective-permute-start(f32[4,10,1,256]{3,2,1,0:T(1,128)S(1)} %get-tuple-element.19), channel_id=1, source_target_pairs={{0,1},{1,2},{2,3},{3,4},{4,5},{5,6},{6,7},{7,8},{8,9},{9,10},{10,1... | collective-permute-start | bytes 122888 | tf_op jit(solution)/shard_map/ppermute | solution.py:16
  427.4 21.9 %collective-permute-start.16 = (f32[4,1,8,256]{3,2,1,0:T(8,128)S(1)}, f32[4,1,8,256]{3,2,1,0:T(8,128)S(1)}, u32[]{:S(2)}, u32[]{:S(2)}) collective-permute-start(f32[4,1,8,256]{3,2,1,0:T(8,128)S(1)} %get-tuple-element.25), channel_id=1, source_target_pairs={{16,0},{32,16},{48,32},{17,1},{33,17},{49,33},{18,2},{34,18},{50,3... | collective-permute-start | bytes 98312 | tf_op jit(solution)/shard_map/ppermute | solution.py:19
  447.9 4.7 collective-permute-start.17
  452.6 6.0 %collective-permute-start.18 = (f32[4,10,1,256]{3,2,1,0:T(1,128)S(1)}, f32[4,10,1,256]{3,2,1,0:T(1,128)S(1)}, u32[]{:S(2)}, u32[]{:S(2)}) collective-permute-start(f32[4,10,1,256]{3,2,1,0:T(1,128)S(1)} %get-tuple-element.16), channel_id=1, source_target_pairs={{1,0},{2,1},{3,2},{4,3},{5,4},{6,5},{7,6},{8,7},{9,8},{10,9},{11,1... | collective-permute-start | bytes 122888 | tf_op jit(solution)/shard_map/ppermute | solution.py:19
  456.7 10.8 %collective-permute-start.19 = (f32[4,10,1,256]{3,2,1,0:T(1,128)S(1)}, f32[4,10,1,256]{3,2,1,0:T(1,128)S(1)}, u32[]{:S(2)}, u32[]{:S(2)}) collective-permute-start(f32[4,10,1,256]{3,2,1,0:T(1,128)S(1)} %get-tuple-element.17), channel_id=1, source_target_pairs={{0,1},{1,2},{2,3},{3,4},{4,5},{5,6},{6,7},{7,8},{8,9},{9,10},{10,1... | collective-permute-start | bytes 122888 | tf_op jit(solution)/shard_map/ppermute | solution.py:16
  467.7 4.7 collective-permute-start.20
  471.1 5.0 collective-permute-start.21
  476.2 5.3 collective-permute-start.22
  478.1 11.3 %collective-permute-start.23 = (f32[8,10,1,256]{3,2,1,0:T(1,128)S(1)}, f32[8,10,1,256]{3,2,1,0:T(1,128)S(1)}, u32[]{:S(2)}, u32[]{:S(2)}) collective-permute-start(f32[8,10,1,256]{3,2,1,0:T(1,128)S(1)} %get-tuple-element.13), channel_id=1, source_target_pairs={{0,1},{1,2},{2,3},{3,4},{4,5},{5,6},{6,7},{7,8},{8,9},{9,10},{10,1... | collective-permute-start | bytes 245768 | tf_op jit(solution)/shard_map/ppermute | solution.py:16
